TPU v7x, 32 devices: a whole 2x2x4 slice. The times are simulated.
32 devices in a mesh: groups: 2 (over y), epoch: 4 (over z), space: 2 (over x), sub: 2 (over core).
Axes of the slice: x: 2, y: 2, z: 4, core: 2. Of those that a mesh axis runs over, the one named last changes fastest.
Arguments:
- slc: bfloat16 [2, 64, 128, 1024], P(None, ('groups', 'epoch'), 'space', 'sub'), parts along dimension 1, may hold values from -8 to 8
- offsets: int32 [64, 4], P(('groups', 'epoch')), parts along dimension 0, may hold values from 1 to 8, as said below
- weights: float32 [64, 4], P(('groups', 'epoch')), parts along dimension 0, may hold values from 0.3 to 3
- estimate: float32 [64, 32, 1024], P(('groups', 'epoch'), 'space', 'sub'), parts along dimension 0, may hold values from -2 to 2
- direction: float32 [64, 32, 1024], P(('groups', 'epoch'), 'space', 'sub'), parts along dimension 0, may hold values from -2 to 2
- prev_mean: float32 [1], replicated, may hold values from 0.05 to 0.5
Outputs:
- new_estimate: float32 [64, 32, 1024], P(('groups', 'epoch'), 'space', 'sub'), parts along dimension 0
- new_direction: float32 [64, 32, 1024], P(('groups', 'epoch'), 'space', 'sub'), parts along dimension 0
There are 2 independent parts, one for each index of `groups`. A program takes and returns all parts, laid end to end along the dimension named above; an argument that names none is the same for every part. Nothing has to cross between parts.
Inputs may be any that keep to these rules, and one draw needn't show every extreme that they name: `offsets`: each row holds 4 different distances; partners wrap past the last epoch to the first.
All inputs are finite; a program needn't handle non-finite values.
Results may differ from a plain program's by a relative error of at most 0.0003.
Values may be sent and summed in bfloat16 or wider, within the bound.
A program may use at most 64 MiB of HBM per device.

v0:
```python
import jax
import jax.numpy as jnp
from jax import lax
from jax.sharding import PartitionSpec as P

SLOTS = 4
OFFS = 8
LOOK = 4
RADIUS = 3
EPSILON = 1e-06


def passed_along(x, axis, by):
    size = lax.axis_size(axis)
    return lax.ppermute(x, axis, [(i, (i + by) % size) for i in range(size)])


def extended_2(block, sides, width):
    for axis, dim in sides:
        count = lax.axis_size(axis)
        forward = [(i, i + 1) for i in range(count - 1)]
        backward = [(target, source) for source, target in forward]
        low = lax.ppermute(
            lax.slice_in_dim(block, block.shape[dim] - width, None, axis=dim), axis, forward
        )
        high = lax.ppermute(lax.slice_in_dim(block, 0, width, axis=dim), axis, backward)
        block = jnp.concatenate([low, block, high], axis=dim)
    return block


def looked_sum(field):
    shape = field.shape
    return jnp.sum(field.reshape(shape[:-2] + (shape[-2] // LOOK, LOOK, shape[-1])), axis=-2)


def window_sum(padded, axis):
    length = padded.shape[axis] - 2 * RADIUS
    total = lax.slice_in_dim(padded, 0, length, axis=axis)
    for shift_at in range(1, 2 * RADIUS + 1):
        total = total + lax.slice_in_dim(padded, shift_at, shift_at + length, axis=axis)
    return total


def on_device(slc, offsets, weights, estimate, direction, prev_mean):
    epochs_here = slc.shape[1]
    look_rows = slc.shape[2] // LOOK
    col_count = slc.shape[3]
    ahead = passed_along(slc, "epoch", -1)
    extended = jnp.concatenate([slc, ahead], axis=1)
    numbers = jnp.arange(epochs_here, dtype=jnp.int32)
    partner = numbers[:, None] + offsets
    own_real = slc[0].astype(jnp.float32)
    own_imag = slc[1].astype(jnp.float32)
    ext_real = extended[0].astype(jnp.float32)
    ext_imag = extended[1].astype(jnp.float32)
    powers = looked_sum(ext_real * ext_real + ext_imag * ext_imag)
    pieces = []
    for slot_index in range(SLOTS):
        mate_real = jnp.take(ext_real, partner[:, slot_index], axis=0)
        mate_imag = jnp.take(ext_imag, partner[:, slot_index], axis=0)
        pieces.append(looked_sum(own_real * mate_real + own_imag * mate_imag))
        pieces.append(looked_sum(own_imag * mate_real - own_real * mate_imag))
    pair_count = epochs_here * 2 * SLOTS
    stacked = jnp.concatenate(
        [jnp.stack(pieces, axis=1).reshape(pair_count, look_rows, col_count), powers], axis=0
    )
    padded = extended_2(stacked, (("space", 1), ("sub", 2)), RADIUS)
    boxed = window_sum(window_sum(padded, 1), 2)
    pair_boxed = boxed[:pair_count].reshape(epochs_here, 2 * SLOTS, look_rows, col_count)
    power_box = boxed[pair_count:]
    coh_real = pair_boxed[:, 0::2]
    coh_imag = pair_boxed[:, 1::2]
    denominator = power_box[:epochs_here, None] * jnp.take(power_box, partner, axis=0) + EPSILON
    coherence = (coh_real * coh_real + coh_imag * coh_imag) / denominator
    observed = coh_imag / jnp.sqrt(denominator)
    est_ahead = passed_along(estimate, "epoch", -1)
    est_extended = jnp.concatenate([estimate, est_ahead], axis=0)
    fitted = estimate[:, None] - jnp.take(est_extended, partner, axis=0)
    factor = weights[:, :, None, None] * coherence
    weighted = factor * (observed - fitted)
    flattened = weighted.reshape(epochs_here * SLOTS, look_rows * col_count)
    selector = (
        jnp.arange(epochs_here + OFFS, dtype=jnp.int32)[:, None] == partner.reshape(1, -1)
    ).astype(jnp.float32)
    gathered = jnp.dot(
        selector, flattened, precision=lax.Precision.HIGHEST, preferred_element_type=jnp.float32
    ).reshape(epochs_here + OFFS, look_rows, col_count)
    own_part = jnp.sum(weighted, axis=1) - gathered[:epochs_here]
    returned = passed_along(-gathered[epochs_here:], "epoch", 1)
    gradient = jnp.concatenate([own_part + returned, own_part[OFFS:]], axis=0)
    cell_count = float(
        epochs_here
        * lax.axis_size("epoch")
        * look_rows
        * lax.axis_size("space")
        * col_count
        * lax.axis_size("sub")
    )
    local_norm = jnp.sum(gradient * gradient)
    local_crossed = jnp.sum(gradient * direction)
    mean_before = prev_mean[0]
    fields_ahead = passed_along(
        jnp.stack([gradient, direction]).astype(jnp.bfloat16), "epoch", -1
    ).astype(jnp.float32)
    grad_extended = jnp.concatenate([gradient, fields_ahead[0]], axis=0)
    old_extended = jnp.concatenate([direction, fields_ahead[1]], axis=0)
    grad_spread = gradient[:, None] - jnp.take(grad_extended, partner, axis=0)
    old_spread = direction[:, None] - jnp.take(old_extended, partner, axis=0)
    totals = lax.psum(
        (
            local_norm,
            local_crossed,
            jnp.sum(factor * grad_spread * grad_spread),
            jnp.sum(factor * grad_spread * old_spread),
            jnp.sum(factor * old_spread * old_spread),
        ),
        ("epoch", "space", "sub"),
    )
    grad_norm, crossed, grad_term, mixed_term, old_term = totals
    momentum = grad_norm / cell_count / mean_before
    new_direction = gradient + momentum * direction
    curvature = grad_term + 2.0 * momentum * mixed_term + momentum * momentum * old_term
    along_sum = grad_norm + momentum * crossed
    step_size = along_sum / curvature
    return (estimate + step_size * new_direction, new_direction)


def solution(mesh):
    return jax.shard_map(
        on_device,
        mesh=mesh,
        in_specs=(
            P(None, ("groups", "epoch"), "space", "sub"),
            P(("groups", "epoch"), None),
            P(("groups", "epoch"), None),
            P(("groups", "epoch"), "space", "sub"),
            P(("groups", "epoch"), "space", "sub"),
            P(),
        ),
        out_specs=(P(("groups", "epoch"), "space", "sub"), P(("groups", "epoch"), "space", "sub")),
        check_vma=False,
    )
```

profile of v0, /device:TPU:0, one launch (start us, length us, event | category | flops | bytes accessed | tf_op | source)
XLA Modules:
  0.0 223.2 jit_solution(3602358008610256752)
XLA Ops:
  0.6 5.1 %collective-permute-start = (bf16[2,8,64,512]{3,2,1,0:T(8,128)(2,1)}, bf16[2,8,64,512]{3,2,1,0:T(8,128)(2,1)S(1)}, u32[]{:S(2)}, u32[]{:S(2)}) collective-permute-start(bf16[2,8,64,512]{3,2,1,0:T(8,128)(2,1)} %param.10), channel_id=1, source_target_pairs={{0,12},{4,0},{8,4},{12,8},{1,13},{5,1},{9,5},{13,9},{2,14},{6,2},{... | collective-permute-start | bytes 3145736 | tf_op jit(solution)/shard_map/ppermute | solution.py:15
  7.8 20.7 %collective-permute-done = bf16[2,8,64,512]{3,2,1,0:T(8,128)(2,1)S(1)} collective-permute-done((bf16[2,8,64,512]{3,2,1,0:T(8,128)(2,1)}, bf16[2,8,64,512]{3,2,1,0:T(8,128)(2,1)S(1)}, u32[]{:S(2)}, u32[]{:S(2)}) %collective-permute-start) | collective-permute-done | bytes 1048608 | tf_op jit(solution)/shard_map/ppermute | solution.py:15
  28.6 1.7 fusion
  30.3 1.9 convert_bitcast_fusion.1
  32.2 3.2 %gather_fusion.5 = f32[8,64,512]{2,1,0:T(8,128)} fusion(f32[16,64,512]{2,1,0:T(8,128)} %get-tuple-element.42, s32[1024]{0:T(1024)S(1)} %get-tuple-element.61), kind=kCustom, calls=%fused_computation.6.clone | custom fusion | bytes 2097184 | tf_op jit(solution)/shard_map/jit(_take)/gather | solution.py:60
  37.0 3.3 %gather_fusion.1 = f32[8,64,512]{2,1,0:T(8,128)} fusion(f32[16,64,512]{2,1,0:T(8,128)} %get-tuple-element.42, s32[1024]{0:T(1024)S(1)} %get-tuple-element.63), kind=kCustom, calls=%fused_computation.2.clone | custom fusion | bytes 2097184 | tf_op jit(solution)/shard_map/jit(_take)/gather | solution.py:60
  41.8 3.2 %gather_fusion.7 = f32[8,64,512]{2,1,0:T(8,128)} fusion(f32[16,64,512]{2,1,0:T(8,128)} %get-tuple-element.42, s32[1024]{0:T(1024)S(1)} %get-tuple-element.60), kind=kCustom, calls=%fused_computation.8.clone | custom fusion | bytes 2097184 | tf_op jit(solution)/shard_map/jit(_take)/gather | solution.py:60
  45.0 1.6 gather_fusion.6
  46.7 3.2 %gather_fusion.3 = f32[8,64,512]{2,1,0:T(8,128)} fusion(f32[16,64,512]{2,1,0:T(8,128)} %get-tuple-element.42, s32[1024]{0:T(1024)S(1)} %get-tuple-element.62), kind=kCustom, calls=%fused_computation.4.clone | custom fusion | bytes 2097184 | tf_op jit(solution)/shard_map/jit(_take)/gather | solution.py:60
  51.4 1.9 add.120
  53.4 4.8 %fusion.7 = (f32[8,64,512]{2,1,0:T(8,128)}, f32[8,64,512]{2,1,0:T(8,128)}, f32[8,64,512]{2,1,0:T(8,128)}, f32[8,64,512]{2,1,0:T(8,128)}) fusion(f32[8,64,512]{2,1,0:T(8,128)} %gather_fusion.5, f32[8,64,512]{2,1,0:T(8,128)} %gather_fusion.4, pred[8]{0:T(512)(128)(4,1)S(1)} %get-tuple-element.52, bf16[2,8,64,512]{3,2,1,0:T(8,128)(2,1)S(1)} %copy-done.1, ...), kind=kLoop, calls=%fused_computation.53 | loop fusion | flops 4718592 | bytes 9437200 | tf_op jit(solution)/shard_map/sub | solution.py:62
  58.2 2.5 %reshape.74 = f32[8,16,4,512]{3,2,1,0:T(4,128)} reshape(f32[8,64,512]{2,1,0:T(8,128)} %get-tuple-element.45) | data formatting | bytes 2097152 | tf_op jit(solution)/shard_map/reshape | solution.py:33
  60.8 2.2 reduce_sum.143
  62.9 1.9 reduce_sum.135
  64.8 2.5 %reshape.75 = f32[8,16,4,512]{3,2,1,0:T(4,128)} reshape(f32[8,64,512]{2,1,0:T(8,128)} %get-tuple-element.46) | data formatting | bytes 2097152 | tf_op jit(solution)/shard_map/reshape | solution.py:33
  67.3 1.9 reduce_sum.136
  69.2 4.8 %fusion.9 = (f32[8,64,512]{2,1,0:T(8,128)}, f32[8,64,512]{2,1,0:T(8,128)}, f32[8,64,512]{2,1,0:T(8,128)}, f32[8,64,512]{2,1,0:T(8,128)}) fusion(f32[8,64,512]{2,1,0:T(8,128)} %gather_fusion.7, f32[8,64,512]{2,1,0:T(8,128)} %gather_fusion.6, pred[8]{0:T(512)(128)(4,1)S(1)} %get-tuple-element.21, bf16[2,8,64,512]{3,2,1,0:T(8,128)(2,1)S(1)} %copy-done.1, ...), kind=kLoop, calls=%fused_computation.55 | loop fusion | flops 4718592 | bytes 9437200 | tf_op jit(solution)/shard_map/sub | solution.py:62
  74.0 2.6 %reshape.76 = f32[8,16,4,512]{3,2,1,0:T(4,128)} reshape(f32[8,64,512]{2,1,0:T(8,128)} %get-tuple-element.43) | data formatting | bytes 2097152 | tf_op jit(solution)/shard_map/reshape | solution.py:33
  76.6 2.6 %reduce_sum.137 = f32[8,16,512]{2,1,0:T(8,128)} reduce(f32[8,16,4,512]{3,2,1,0:T(4,128)} %reshape.76, f32[]{:T(128)} %constant.20.clone.1), dimensions={2}, to_apply=%region_2.4 | reduce | flops 196608 | bytes 1310724 | tf_op jit(solution)/shard_map/reduce_sum | solution.py:33
  80.5 2.7 %reduce_sum.138 = f32[8,16,512]{2,1,0:T(8,128)} reduce(f32[8,16,4,512]{3,2,1,0:T(4,128)} %reshape.77, f32[]{:T(128)} %constant.20.clone.1), dimensions={2}, to_apply=%region_3.5 | reduce | flops 196608 | bytes 1310724 | tf_op jit(solution)/shard_map/reduce_sum | solution.py:33
  83.1 2.5 %reshape.78 = f32[8,16,4,512]{3,2,1,0:T(4,128)} reshape(f32[8,64,512]{2,1,0:T(8,128)} %get-tuple-element.34) | data formatting | bytes 2097152 | tf_op jit(solution)/shard_map/reshape | solution.py:33
  85.7 2.6 %reduce_sum.139 = f32[8,16,512]{2,1,0:T(8,128)} reduce(f32[8,16,4,512]{3,2,1,0:T(4,128)} %reshape.78, f32[]{:T(128)} %constant.20.clone.1), dimensions={2}, to_apply=%region_4.6 | reduce | flops 196608 | bytes 1310724 | tf_op jit(solution)/shard_map/reduce_sum | solution.py:33
  89.5 2.7 %reduce_sum.140 = f32[8,16,512]{2,1,0:T(8,128)} reduce(f32[8,16,4,512]{3,2,1,0:T(4,128)} %reshape.79, f32[]{:T(128)} %constant.20.clone.1), dimensions={2}, to_apply=%region_5.7 | reduce | flops 196608 | bytes 1310724 | tf_op jit(solution)/shard_map/reduce_sum | solution.py:33
  92.2 2.5 %reshape.80 = f32[8,16,4,512]{3,2,1,0:T(4,128)} reshape(f32[8,64,512]{2,1,0:T(8,128)} %get-tuple-element.32) | data formatting | bytes 2097152 | tf_op jit(solution)/shard_map/reshape | solution.py:33
  94.7 2.5 %reduce_sum.141 = f32[8,16,512]{2,1,0:T(8,128)} reduce(f32[8,16,4,512]{3,2,1,0:T(4,128)} %reshape.80, f32[]{:T(128)} %constant.20.clone.1), dimensions={2}, to_apply=%region_6.8 | reduce | flops 196608 | bytes 1310724 | tf_op jit(solution)/shard_map/reduce_sum | solution.py:33
  98.5 2.6 %reduce_sum.142 = f32[8,16,512]{2,1,0:T(8,128)} reduce(f32[8,16,4,512]{3,2,1,0:T(4,128)} %reshape.81, f32[]{:T(128)} %constant.20.clone.1), dimensions={2}, to_apply=%region_7.9 | reduce | flops 196608 | bytes 1310724 | tf_op jit(solution)/shard_map/reduce_sum | solution.py:33
  105.5 5.9 %collective-permute-start.1 = (f32[80,3,512]{2,0,1:T(8,128)}, f32[80,3,512]{2,0,1:T(8,128)}, u32[]{:S(2)}, u32[]{:S(2)}) collective-permute-start(f32[80,3,512]{2,0,1:T(8,128)} %copy.55), channel_id=1, source_target_pairs={{0,2},{1,3},{4,6},{5,7},{8,10},{9,11},{12,14},{13,15},{16,18},{17,... | collective-permute-start | bytes 1474568 | tf_op jit(solution)/shard_map/ppermute | solution.py:23
  111.4 4.2 %collective-permute-start.5 = (f32[8,16,512]{2,1,0:T(8,128)S(1)}, f32[8,16,512]{2,1,0:T(8,128)}, u32[]{:S(2)}, u32[]{:S(2)}) collective-permute-start(f32[8,16,512]{2,1,0:T(8,128)S(1)} %copy-done.8), channel_id=1, source_target_pairs={{0,12},{4,0},{8,4},{12,8},{1,13},{5,1},{9,5},{13,9},{2,14},{6,2},{... | collective-permute-start | bytes 786440 | tf_op jit(solution)/shard_map/ppermute | solution.py:15
  118.5 1.7 collective-permute-done.1
  121.6 1.9 pad_maximum_fusion.4
  123.5 2.2 copy.60
  126.9 2.2 copy.59
  129.1 4.2 %collective-permute-start.3 = (f32[80,22,3]{0,1,2:T(8,128)}, f32[80,22,3]{0,1,2:T(8,128)}, u32[]{:S(2)}, u32[]{:S(2)}) collective-permute-start(f32[80,22,3]{0,1,2:T(8,128)} %copy.59), channel_id=1, source_target_pairs={{0,1},{2,3},{4,5},{6,7},{8,9},{10,11},{12,13},{14,15},{16,17},{18,... | collective-permute-start | bytes 63368 | tf_op jit(solution)/shard_map/ppermute | solution.py:23
  133.3 1.8 pad_maximum_fusion.7
  135.1 2.7 %gather_fusion.9 = f32[32,16,512]{2,1,0:T(8,128)} fusion(f32[16,16,512]{2,1,0:T(8,128)} %pad_maximum_fusion.7, s32[1024]{0:T(1024)S(1)} %pad_clamp_fusion), kind=kCustom, calls=%fused_computation.9.clone | custom fusion | bytes 2097280 | tf_op jit(solution)/shard_map/jit(_take)/gather | solution.py:78
  137.8 2.1 copy.62
  139.9 2.1 copy.61
  142.0 6.8 %pad_maximum_fusion = f32[80,22,518]{2,1,0:T(8,128)S(1)} fusion(f32[80,22,3]{2,1,0:T(8,128)} %copy.62, f32[80,3,512]{2,1,0:T(4,128)S(1)} %copy.58, f32[16,16,512]{2,1,0:T(8,128)S(1)} %copy-done.2, f32[64,16,512]{2,1,0:T(8,128)S(1)} %bitcast.80, f32[80,3,512]{2,1,0:T(4,128)} %copy-done.3, f32[80,22,3]{2,1,0:T(8,128)} %copy.61), kind=kLoop, calls=%fused_computation.12 | loop fusion | flops 4558400 | bytes 7293440 | tf_op jit(solution)/shard_map/concatenate | solution.py:27
  148.8 2.0 slice_add_fusion
  150.8 4.2 %slice_add_fusion.6 = f32[80,16,512]{2,1,0:T(8,128)S(1)} fusion(f32[80,16,518]{2,1,0:T(8,128)S(1)} %slice_add_fusion), kind=kLoop, calls=%fused_computation.39 | loop fusion | flops 3932160 | bytes 20971520 | tf_op jit(solution)/shard_map/add | solution.py:40
  155.0 1.6 slice.190
  157.3 1.6 gather_fusion.8
  158.9 2.8 %fusion.17 = (f32[8,16,512]{2,1,0:T(8,128)S(1)}, f32[8,4,16,512]{3,2,1,0:T(8,128)S(1)}, f32[8,4,16,512]{3,2,1,0:T(8,128)S(1)}) fusion(f32[8,16,512]{2,1,0:T(8,128)S(1)} %copy-done.8, pred[8,4]{1,0:T(8,128)(4,1)S(1)} %copy.63, f32[8,16,512]{2,1,0:T(8,128)S(1)} %slice-done, f32[8,8,16,512]{3,2,1,0:T(8,128)} %bitcast.81, f32[8,4]{1,0:T(8,128)S(1)} %copy.54, ...), kind=kLoop, calls=%fused_computation.116 | loop fusion | flops 3604480 | bytes 7078048 | tf_op jit(solution)/shard_map/reduce_sum | solution.py:88
  163.4 9.1 %collective-permute-done.6 = f32[8,16,512]{2,1,0:T(8,128)S(1)} collective-permute-done((f32[8,16,512]{2,1,0:T(8,128)S(1)}, f32[8,16,512]{2,1,0:T(8,128)S(1)}, u32[]{:S(2)}, u32[]{:S(2)}) %collective-permute-start.6) | collective-permute-done | bytes 262176 | tf_op jit(solution)/shard_map/ppermute | solution.py:15
  173.5 1.7 collective-permute-start.7
  175.9 4.0 %collective-permute-done.7 = bf16[2,8,16,512]{3,2,1,0:T(8,128)(2,1)S(1)} collective-permute-done((bf16[2,8,16,512]{3,2,1,0:T(8,128)(2,1)S(1)}, bf16[2,8,16,512]{3,2,1,0:T(8,128)(2,1)S(1)}, u32[]{:S(2)}, u32[]{:S(2)}) %collective-permute-start.7) | collective-permute-done | bytes 262176 | tf_op jit(solution)/shard_map/ppermute | solution.py:15
  184.0 2.4 %fusion.1 = (f32[]{:T(128)}, f32[]{:T(128)}, f32[]{:T(128)}) fusion(f32[8,4,16,512]{3,2,1,0:T(8,128)S(1)} %get-tuple-element.20, f32[8,4,16,512]{3,2,1,0:T(8,128)S(1)} %bitcast.82, f32[8,16,512]{2,1,0:T(8,128)S(1)} %copy-done.7, pred[8,4]{1,0:T(8,128)(4,1)S(1)} %copy.63, f32[8,4,16,512]{3,2,1,0:T(8,128)} %bitcast.83, f32[8,16,512]{2,1,0:T(8,128)S(1)} %get-tuple-element.17), kind=kLoop, calls=%fused_computation.47 | loop fusion | flops 3145725 | bytes 3670060 | tf_op jit(solution)/shard_map/reduce_sum | solution.py:115
  186.4 32.0 %all-reduce = (f32[]{:T(128)}, f32[]{:T(128)}, f32[]{:T(128)}, f32[]{:T(128)}, f32[]{:T(128)}) all-reduce(f32[]{:T(128)} %get-tuple-element.8, f32[]{:T(128)} %get-tuple-element.7, f32[]{:T(128)} %get-tuple-element.6, f32[]{:T(128)} %get-tuple-element.5, ...), channel_id=1, replica_groups=mesh['groups'=2,'epoch'=4,'space'=2,'sub'=2] {'epoch','space','sub'}, use_global_device_ids=true, to_apply=%region_11.14 | all-reduce | flops 5 | bytes 40 | tf_op jit(solution)/shard_map/psum | solution.py:109
  (89 shorter events, 28.7 us)
Async XLA Ops:
  0.6 27.9 %collective-permute-start = (bf16[2,8,64,512]{3,2,1,0:T(8,128)(2,1)}, bf16[2,8,64,512]{3,2,1,0:T(8,128)(2,1)S(1)}, u32[]{:S(2)}, u32[]{:S(2)}) collective-permute-start(bf16[2,8,64,512]{3,2,1,0:T(8,128)(2,1)} %param.10), channel_id=1, source_target_pairs={{0,12},{4,0},{8,4},{12,8},{1,13},{5,1},{9,5},{13,9},{2,14},{6,2},{... | collective-permute-start | bytes 3145736 | tf_op jit(solution)/shard_map/ppermute | solution.py:15
  51.4 2.0 copy-start.1
  74.0 5.2 %copy-start.6 = (f32[8,64,512]{2,1,0:T(8,128)S(1)}, f32[8,64,512]{2,1,0:T(8,128)}, u32[]{:S(2)}) copy-start(f32[8,64,512]{2,1,0:T(8,128)} %get-tuple-element.44) | copy-start | bytes 3145732
  80.5 7.7 %copy-start.4 = (f32[8,64,512]{2,1,0:T(8,128)S(1)}, f32[8,64,512]{2,1,0:T(8,128)}, u32[]{:S(2)}) copy-start(f32[8,64,512]{2,1,0:T(8,128)} %get-tuple-element.33) | copy-start | bytes 3145732
  89.5 7.7 %copy-start.5 = (f32[8,64,512]{2,1,0:T(8,128)S(1)}, f32[8,64,512]{2,1,0:T(8,128)}, u32[]{:S(2)}) copy-start(f32[8,64,512]{2,1,0:T(8,128)} %get-tuple-element.31) | copy-start | bytes 3145732
  98.5 3.8 %copy-start.9 = (f32[8,16,512]{2,1,0:T(8,128)S(1)}, f32[8,16,512]{2,1,0:T(8,128)}, u32[]{:S(2)}) copy-start(f32[8,16,512]{2,1,0:T(8,128)} %reduce_sum.138) | copy-start | bytes 786436
  98.5 3.8 %copy-start.10 = (f32[8,16,512]{2,1,0:T(8,128)S(1)}, f32[8,16,512]{2,1,0:T(8,128)}, u32[]{:S(2)}) copy-start(f32[8,16,512]{2,1,0:T(8,128)} %reduce_sum.139) | copy-start | bytes 786436
  101.2 1.2 copy-start.11
  101.2 1.2 copy-start.12
  101.2 1.3 copy-start.13
  101.2 1.4 copy-start.2
  102.9 8.6 %copy-start.8 = (f32[8,16,512]{2,1,0:T(8,128)S(1)}, f32[8,16,512]{2,1,0:T(8,128)}, u32[]{:S(2)}) copy-start(f32[8,16,512]{2,1,0:T(8,128)} %param.13) | copy-start | bytes 786436
  102.9 12.8 %copy-start.14 = (s32[8,4]{0,1:T(4,128)S(1)}, s32[8,4]{0,1:T(4,128)}, u32[]{:S(2)}) copy-start(s32[8,4]{0,1:T(4,128)} %param.11) | copy-start | bytes 388
  102.9 12.9 %copy-start.15 = (f32[8,4]{0,1:T(4,128)S(1)}, f32[8,4]{0,1:T(4,128)}, u32[]{:S(2)}) copy-start(f32[8,4]{0,1:T(4,128)} %param.12) | copy-start | bytes 388
  103.1 14.1 %collective-permute-start.2 = (f32[80,3,512]{2,0,1:T(8,128)S(1)}, f32[80,3,512]{2,0,1:T(8,128)}, u32[]{:S(2)}, u32[]{:S(2)}) collective-permute-start(f32[80,3,512]{2,0,1:T(8,128)S(1)} %copy.56), channel_id=1, source_target_pairs={{2,0},{3,1},{6,4},{7,5},{10,8},{11,9},{14,12},{15,13},{18,16},{19,... | collective-permute-start | bytes 1474568 | tf_op jit(solution)/shard_map/ppermute | solution.py:26
  105.5 14.8 %collective-permute-start.1 = (f32[80,3,512]{2,0,1:T(8,128)}, f32[80,3,512]{2,0,1:T(8,128)}, u32[]{:S(2)}, u32[]{:S(2)}) collective-permute-start(f32[80,3,512]{2,0,1:T(8,128)} %copy.55), channel_id=1, source_target_pairs={{0,2},{1,3},{4,6},{5,7},{8,10},{9,11},{12,14},{13,15},{16,18},{17,... | collective-permute-start | bytes 1474568 | tf_op jit(solution)/shard_map/ppermute | solution.py:23
  111.4 21.9 %collective-permute-start.5 = (f32[8,16,512]{2,1,0:T(8,128)S(1)}, f32[8,16,512]{2,1,0:T(8,128)}, u32[]{:S(2)}, u32[]{:S(2)}) collective-permute-start(f32[8,16,512]{2,1,0:T(8,128)S(1)} %copy-done.8), channel_id=1, source_target_pairs={{0,12},{4,0},{8,4},{12,8},{1,13},{5,1},{9,5},{13,9},{2,14},{6,2},{... | collective-permute-start | bytes 786440 | tf_op jit(solution)/shard_map/ppermute | solution.py:15
  121.6 1.9 copy-start.3
  125.7 12.2 %collective-permute-start.4 = (f32[80,22,3]{0,1,2:T(8,128)}, f32[80,22,3]{0,1,2:T(8,128)}, u32[]{:S(2)}, u32[]{:S(2)}) collective-permute-start(f32[80,22,3]{0,1,2:T(8,128)} %copy.60), channel_id=1, source_target_pairs={{1,0},{3,2},{5,4},{7,6},{9,8},{11,10},{13,12},{15,14},{17,16},{19,... | collective-permute-start | bytes 63368 | tf_op jit(solution)/shard_map/ppermute | solution.py:26
  129.1 10.8 %collective-permute-start.3 = (f32[80,22,3]{0,1,2:T(8,128)}, f32[80,22,3]{0,1,2:T(8,128)}, u32[]{:S(2)}, u32[]{:S(2)}) collective-permute-start(f32[80,22,3]{0,1,2:T(8,128)} %copy.59), channel_id=1, source_target_pairs={{0,1},{2,3},{4,5},{6,7},{8,9},{10,11},{12,13},{14,15},{16,17},{18,... | collective-permute-start | bytes 63368 | tf_op jit(solution)/shard_map/ppermute | solution.py:23
  155.0 2.2 copy-start
  157.2 1.6 slice-start
  162.3 10.4 %copy-start.7 = (f32[8,16,512]{2,1,0:T(8,128)S(1)}, f32[8,16,512]{2,1,0:T(8,128)}, u32[]{:S(2)}) copy-start(f32[8,16,512]{2,1,0:T(8,128)} %param.14) | copy-start | bytes 786436
  163.0 9.5 %collective-permute-start.6 = (f32[8,16,512]{2,1,0:T(8,128)S(1)}, f32[8,16,512]{2,1,0:T(8,128)S(1)}, u32[]{:S(2)}, u32[]{:S(2)}) collective-permute-start(f32[8,16,512]{2,1,0:T(8,128)S(1)} %copy.69), channel_id=1, source_target_pairs={{0,4},{4,8},{8,12},{12,0},{1,5},{5,9},{9,13},{13,1},{2,6},{6,10},{... | collective-permute-start | bytes 786440 | tf_op jit(solution)/shard_map/ppermute | solution.py:15
  173.5 6.4 %collective-permute-start.7 = (bf16[2,8,16,512]{3,2,1,0:T(8,128)(2,1)S(1)}, bf16[2,8,16,512]{3,2,1,0:T(8,128)(2,1)S(1)}, u32[]{:S(2)}, u32[]{:S(2)}) collective-permute-start(bf16[2,8,16,512]{3,2,1,0:T(8,128)(2,1)S(1)} %pad_maximum_fusion.10), channel_id=1, source_target_pairs={{0,12},{4,0},{8,4},{12,8},{1,13},{5,1},{9,5},{13,9},{2,14},{6,2},{... | collective-permute-start | bytes 786440 | tf_op jit(solution)/shard_map/ppermute | solution.py:15
where the time goes:
time: 225 us; the launch traced here: 223 us
  local copies, waits for them, and re-layouts  63.5 us (28%)
  other arithmetic  60.6 us (27%)
  waiting for transfers between devices  36.6 us (16%)
  blocking collectives  32 us (14%)
  starting transfers between devices  24.4 us (11%)
  between operations  5.64 us (3%)
    ppermute x4, waiting for transfers between devices, passed_along(): return lax.ppermute(x, axis, [(i, (i + by) % size) for i in range(size)])  33.8 us
    psum x1, blocking collectives, on_device(): lax.psum((local_norm, local_crossed, jnp.sum(factor * grad_spread * grad_...  32 us
    reduce_sum x9, other arithmetic, looked_sum(): jnp.sum(field.reshape(shape[:-2] + (shape[-2] // LOOK, LOOK, shape[-1])),...  21.5 us
    reshape x8, local copies, waits for them, and re-layouts, looked_sum(): field.reshape(shape[:-2] + (shape[-2] // LOOK, LOOK, shape[-1]))  16.5 us
    gather x4, local copies, waits for them, and re-layouts, on_device(): mate_imag = jnp.take(ext_imag, partner[:, slot_index], axis=0)  12.8 us
    ppermute x4, starting transfers between devices, passed_along(): return lax.ppermute(x, axis, [(i, (i + by) % size) for i in range(size)])  11.5 us
    ppermute x2, starting transfers between devices, extended_2(): lax.ppermute(lax.slice_in_dim(block, block.shape[dim] - width, None, axis...  10.2 us
    sub x2, other arithmetic, on_device(): pieces.append(looked_sum(own_imag * mate_real - own_real * mate_imag))  9.68 us
  transfers between devices with their start and end apart: 8, of which 5 were waited for; matrix products, arithmetic and copies ran while one was open for 8% of the time, Pallas kernels for 0%

commit v1 on v0

--- a/solution.py
+++ b/solution.py
@@ -107,14 +107,17 @@
     grad_spread = gradient[:, None] - jnp.take(grad_extended, partner, axis=0)
     old_spread = direction[:, None] - jnp.take(old_extended, partner, axis=0)
     totals = lax.psum(
-        (
-            local_norm,
-            local_crossed,
-            jnp.sum(factor * grad_spread * grad_spread),
-            jnp.sum(factor * grad_spread * old_spread),
-            jnp.sum(factor * old_spread * old_spread),
+        lax.psum(
+            (
+                local_norm,
+                local_crossed,
+                jnp.sum(factor * grad_spread * grad_spread),
+                jnp.sum(factor * grad_spread * old_spread),
+                jnp.sum(factor * old_spread * old_spread),
+            ),
+            "epoch",
         ),
-        ("epoch", "space", "sub"),
+        ("space", "sub"),
     )
     grad_norm, crossed, grad_term, mixed_term, old_term = totals
     momentum = grad_norm / cell_count / mean_before

time: 225 us -> 212 us (0.942)
  blocking collectives: 32 us -> 19.2 us
    psum x1, blocking collectives: 32 us -> 12.5 us  [on_device(): lax.psum((local_norm, local_crossed, jnp.sum(factor * grad_spread * grad_...]
    psum x0 -> x1, blocking collectives: none -> 6.71 us  [on_device(): lax.psum(lax.psum((local_norm, local_crossed, jnp.sum(factor * grad_sprea...]
  transfers between devices with their start and end apart: 8 -> 8, of which waited for: 5 -> 5; matrix products, arithmetic and copies ran while one was open for 8% -> 9% of each run, Pallas kernels for 0% -> 0%
where the time goes in v1:
time: 212 us; the launch traced here: 210 us
  local copies, waits for them, and re-layouts  63.5 us (30%)
  other arithmetic  60.6 us (29%)
  waiting for transfers between devices  36.6 us (17%)
  starting transfers between devices  24.4 us (12%)
  blocking collectives  19.2 us (9%)
  between operations  5.56 us (3%)
    ppermute x4, waiting for transfers between devices, passed_along(): return lax.ppermute(x, axis, [(i, (i + by) % size) for i in range(size)])  33.8 us
    reduce_sum x9, other arithmetic, looked_sum(): jnp.sum(field.reshape(shape[:-2] + (shape[-2] // LOOK, LOOK, shape[-1])),...  21.5 us
    reshape x8, local copies, waits for them, and re-layouts, looked_sum(): field.reshape(shape[:-2] + (shape[-2] // LOOK, LOOK, shape[-1]))  16.5 us
    gather x4, local copies, waits for them, and re-layouts, on_device(): mate_imag = jnp.take(ext_imag, partner[:, slot_index], axis=0)  12.8 us
    psum x1, blocking collectives, on_device(): lax.psum((local_norm, local_crossed, jnp.sum(factor * grad_spread * grad_...  12.5 us
    ppermute x4, starting transfers between devices, passed_along(): return lax.ppermute(x, axis, [(i, (i + by) % size) for i in range(size)])  11.5 us
    ppermute x2, starting transfers between devices, extended_2(): lax.ppermute(lax.slice_in_dim(block, block.shape[dim] - width, None, axis...  10.2 us
    sub x2, other arithmetic, on_device(): pieces.append(looked_sum(own_imag * mate_real - own_real * mate_imag))  9.68 us
  transfers between devices with their start and end apart: 8, of which 5 were waited for; matrix products, arithmetic and copies ran while one was open for 9% of the time, Pallas kernels for 0%

profile of v1, /device:TPU:0, one launch (start us, length us, event | category | flops | bytes accessed | tf_op | source)
XLA Modules:
  0.0 210.4 jit_solution(14228615158309159108)
XLA Ops:
  0.6 5.1 %collective-permute-start = (bf16[2,8,64,512]{3,2,1,0:T(8,128)(2,1)}, bf16[2,8,64,512]{3,2,1,0:T(8,128)(2,1)S(1)}, u32[]{:S(2)}, u32[]{:S(2)}) collective-permute-start(bf16[2,8,64,512]{3,2,1,0:T(8,128)(2,1)} %param.10), channel_id=1, source_target_pairs={{0,12},{4,0},{8,4},{12,8},{1,13},{5,1},{9,5},{13,9},{2,14},{6,2},{... | collective-permute-start | bytes 3145736 | tf_op jit(solution)/shard_map/ppermute | solution.py:15
  7.8 20.7 %collective-permute-done = bf16[2,8,64,512]{3,2,1,0:T(8,128)(2,1)S(1)} collective-permute-done((bf16[2,8,64,512]{3,2,1,0:T(8,128)(2,1)}, bf16[2,8,64,512]{3,2,1,0:T(8,128)(2,1)S(1)}, u32[]{:S(2)}, u32[]{:S(2)}) %collective-permute-start) | collective-permute-done | bytes 1048608 | tf_op jit(solution)/shard_map/ppermute | solution.py:15
  28.6 1.7 fusion
  30.3 1.9 convert_bitcast_fusion.1
  32.2 3.2 %gather_fusion.5 = f32[8,64,512]{2,1,0:T(8,128)} fusion(f32[16,64,512]{2,1,0:T(8,128)} %get-tuple-element.47, s32[1024]{0:T(1024)S(1)} %get-tuple-element.66), kind=kCustom, calls=%fused_computation.6.clone | custom fusion | bytes 2097184 | tf_op jit(solution)/shard_map/jit(_take)/gather | solution.py:60
  37.0 3.3 %gather_fusion.1 = f32[8,64,512]{2,1,0:T(8,128)} fusion(f32[16,64,512]{2,1,0:T(8,128)} %get-tuple-element.47, s32[1024]{0:T(1024)S(1)} %get-tuple-element.68), kind=kCustom, calls=%fused_computation.2.clone | custom fusion | bytes 2097184 | tf_op jit(solution)/shard_map/jit(_take)/gather | solution.py:60
  41.8 3.2 %gather_fusion.7 = f32[8,64,512]{2,1,0:T(8,128)} fusion(f32[16,64,512]{2,1,0:T(8,128)} %get-tuple-element.47, s32[1024]{0:T(1024)S(1)} %get-tuple-element.65), kind=kCustom, calls=%fused_computation.8.clone | custom fusion | bytes 2097184 | tf_op jit(solution)/shard_map/jit(_take)/gather | solution.py:60
  45.0 1.6 gather_fusion.6
  46.7 3.2 %gather_fusion.3 = f32[8,64,512]{2,1,0:T(8,128)} fusion(f32[16,64,512]{2,1,0:T(8,128)} %get-tuple-element.47, s32[1024]{0:T(1024)S(1)} %get-tuple-element.67), kind=kCustom, calls=%fused_computation.4.clone | custom fusion | bytes 2097184 | tf_op jit(solution)/shard_map/jit(_take)/gather | solution.py:60
  51.4 1.9 add.130
  53.4 4.8 %fusion.7 = (f32[8,64,512]{2,1,0:T(8,128)}, f32[8,64,512]{2,1,0:T(8,128)}, f32[8,64,512]{2,1,0:T(8,128)}, f32[8,64,512]{2,1,0:T(8,128)}) fusion(f32[8,64,512]{2,1,0:T(8,128)} %gather_fusion.5, f32[8,64,512]{2,1,0:T(8,128)} %gather_fusion.4, pred[8]{0:T(512)(128)(4,1)S(1)} %get-tuple-element.57, bf16[2,8,64,512]{3,2,1,0:T(8,128)(2,1)S(1)} %copy-done.1, ...), kind=kLoop, calls=%fused_computation.53 | loop fusion | flops 4718592 | bytes 9437200 | tf_op jit(solution)/shard_map/sub | solution.py:62
  58.2 2.5 %reshape.74 = f32[8,16,4,512]{3,2,1,0:T(4,128)} reshape(f32[8,64,512]{2,1,0:T(8,128)} %get-tuple-element.50) | data formatting | bytes 2097152 | tf_op jit(solution)/shard_map/reshape | solution.py:33
  60.8 2.2 %reduce_sum.143 = f32[16,16,512]{2,1,0:T(8,128)} reduce(f32[16,16,4,512]{3,2,1,0:T(4,128)S(1)} %add.130, f32[]{:T(128)} %constant.20.clone.1), dimensions={2}, to_apply=%region_8.10 | reduce | flops 393216 | bytes 2621444 | tf_op jit(solution)/shard_map/reduce_sum | solution.py:33
  62.9 1.9 reduce_sum.135
  64.8 2.5 %reshape.75 = f32[8,16,4,512]{3,2,1,0:T(4,128)} reshape(f32[8,64,512]{2,1,0:T(8,128)} %get-tuple-element.51) | data formatting | bytes 2097152 | tf_op jit(solution)/shard_map/reshape | solution.py:33
  67.3 1.9 reduce_sum.136
  69.2 4.8 %fusion.9 = (f32[8,64,512]{2,1,0:T(8,128)}, f32[8,64,512]{2,1,0:T(8,128)}, f32[8,64,512]{2,1,0:T(8,128)}, f32[8,64,512]{2,1,0:T(8,128)}) fusion(f32[8,64,512]{2,1,0:T(8,128)} %gather_fusion.7, f32[8,64,512]{2,1,0:T(8,128)} %gather_fusion.6, pred[8]{0:T(512)(128)(4,1)S(1)} %get-tuple-element.26, bf16[2,8,64,512]{3,2,1,0:T(8,128)(2,1)S(1)} %copy-done.1, ...), kind=kLoop, calls=%fused_computation.55 | loop fusion | flops 4718592 | bytes 9437200 | tf_op jit(solution)/shard_map/sub | solution.py:62
  74.0 2.6 %reshape.76 = f32[8,16,4,512]{3,2,1,0:T(4,128)} reshape(f32[8,64,512]{2,1,0:T(8,128)} %get-tuple-element.48) | data formatting | bytes 2097152 | tf_op jit(solution)/shard_map/reshape | solution.py:33
  76.6 2.6 %reduce_sum.137 = f32[8,16,512]{2,1,0:T(8,128)} reduce(f32[8,16,4,512]{3,2,1,0:T(4,128)} %reshape.76, f32[]{:T(128)} %constant.20.clone.1), dimensions={2}, to_apply=%region_2.4 | reduce | flops 196608 | bytes 1310724 | tf_op jit(solution)/shard_map/reduce_sum | solution.py:33
  80.5 2.7 %reduce_sum.138 = f32[8,16,512]{2,1,0:T(8,128)} reduce(f32[8,16,4,512]{3,2,1,0:T(4,128)} %reshape.77, f32[]{:T(128)} %constant.20.clone.1), dimensions={2}, to_apply=%region_3.5 | reduce | flops 196608 | bytes 1310724 | tf_op jit(solution)/shard_map/reduce_sum | solution.py:33
  83.1 2.5 %reshape.78 = f32[8,16,4,512]{3,2,1,0:T(4,128)} reshape(f32[8,64,512]{2,1,0:T(8,128)} %get-tuple-element.39) | data formatting | bytes 2097152 | tf_op jit(solution)/shard_map/reshape | solution.py:33
  85.7 2.6 %reduce_sum.139 = f32[8,16,512]{2,1,0:T(8,128)} reduce(f32[8,16,4,512]{3,2,1,0:T(4,128)} %reshape.78, f32[]{:T(128)} %constant.20.clone.1), dimensions={2}, to_apply=%region_4.6 | reduce | flops 196608 | bytes 1310724 | tf_op jit(solution)/shard_map/reduce_sum | solution.py:33
  89.5 2.7 %reduce_sum.140 = f32[8,16,512]{2,1,0:T(8,128)} reduce(f32[8,16,4,512]{3,2,1,0:T(4,128)} %reshape.79, f32[]{:T(128)} %constant.20.clone.1), dimensions={2}, to_apply=%region_5.7 | reduce | flops 196608 | bytes 1310724 | tf_op jit(solution)/shard_map/reduce_sum | solution.py:33
  92.2 2.5 %reshape.80 = f32[8,16,4,512]{3,2,1,0:T(4,128)} reshape(f32[8,64,512]{2,1,0:T(8,128)} %get-tuple-element.37) | data formatting | bytes 2097152 | tf_op jit(solution)/shard_map/reshape | solution.py:33
  94.7 2.5 %reduce_sum.141 = f32[8,16,512]{2,1,0:T(8,128)} reduce(f32[8,16,4,512]{3,2,1,0:T(4,128)} %reshape.80, f32[]{:T(128)} %constant.20.clone.1), dimensions={2}, to_apply=%region_6.8 | reduce | flops 196608 | bytes 1310724 | tf_op jit(solution)/shard_map/reduce_sum | solution.py:33
  98.5 2.6 %reduce_sum.142 = f32[8,16,512]{2,1,0:T(8,128)} reduce(f32[8,16,4,512]{3,2,1,0:T(4,128)} %reshape.81, f32[]{:T(128)} %constant.20.clone.1), dimensions={2}, to_apply=%region_7.9 | reduce | flops 196608 | bytes 1310724 | tf_op jit(solution)/shard_map/reduce_sum | solution.py:33
  105.5 5.9 %collective-permute-start.1 = (f32[80,3,512]{2,0,1:T(8,128)}, f32[80,3,512]{2,0,1:T(8,128)}, u32[]{:S(2)}, u32[]{:S(2)}) collective-permute-start(f32[80,3,512]{2,0,1:T(8,128)} %copy.55), channel_id=1, source_target_pairs={{0,2},{1,3},{4,6},{5,7},{8,10},{9,11},{12,14},{13,15},{16,18},{17,... | collective-permute-start | bytes 1474568 | tf_op jit(solution)/shard_map/ppermute | solution.py:23
  111.4 4.2 %collective-permute-start.5 = (f32[8,16,512]{2,1,0:T(8,128)S(1)}, f32[8,16,512]{2,1,0:T(8,128)}, u32[]{:S(2)}, u32[]{:S(2)}) collective-permute-start(f32[8,16,512]{2,1,0:T(8,128)S(1)} %copy-done.8), channel_id=1, source_target_pairs={{0,12},{4,0},{8,4},{12,8},{1,13},{5,1},{9,5},{13,9},{2,14},{6,2},{... | collective-permute-start | bytes 786440 | tf_op jit(solution)/shard_map/ppermute | solution.py:15
  118.5 1.7 collective-permute-done.1
  121.6 1.9 pad_maximum_fusion.4
  123.5 2.2 %copy.60 = f32[80,22,3]{0,1,2:T(8,128)} copy(f32[80,22,3]{2,1,0:T(8,128)} %get-tuple-element.35) | data formatting | bytes 42240 | tf_op jit(solution)/shard_map/slice | solution.py:26
  126.9 2.2 %copy.59 = f32[80,22,3]{0,1,2:T(8,128)} copy(f32[80,22,3]{2,1,0:T(8,128)} %get-tuple-element.34) | data formatting | bytes 42240 | tf_op jit(solution)/shard_map/slice | solution.py:24
  129.1 4.2 %collective-permute-start.3 = (f32[80,22,3]{0,1,2:T(8,128)}, f32[80,22,3]{0,1,2:T(8,128)}, u32[]{:S(2)}, u32[]{:S(2)}) collective-permute-start(f32[80,22,3]{0,1,2:T(8,128)} %copy.59), channel_id=1, source_target_pairs={{0,1},{2,3},{4,5},{6,7},{8,9},{10,11},{12,13},{14,15},{16,17},{18,... | collective-permute-start | bytes 63368 | tf_op jit(solution)/shard_map/ppermute | solution.py:23
  133.3 1.8 pad_maximum_fusion.7
  135.1 2.7 %gather_fusion.9 = f32[32,16,512]{2,1,0:T(8,128)} fusion(f32[16,16,512]{2,1,0:T(8,128)} %pad_maximum_fusion.7, s32[1024]{0:T(1024)S(1)} %pad_clamp_fusion), kind=kCustom, calls=%fused_computation.9.clone | custom fusion | bytes 2097280 | tf_op jit(solution)/shard_map/jit(_take)/gather | solution.py:78
  137.8 2.1 copy.62
  139.9 2.1 %copy.61 = f32[80,22,3]{2,1,0:T(8,128)} copy(f32[80,22,3]{0,1,2:T(8,128)} %collective-permute-done.3) | data formatting | bytes 42240 | tf_op jit(solution)/shard_map/ppermute | solution.py:23
  142.0 6.8 %pad_maximum_fusion = f32[80,22,518]{2,1,0:T(8,128)S(1)} fusion(f32[80,22,3]{2,1,0:T(8,128)} %copy.62, f32[80,3,512]{2,1,0:T(4,128)S(1)} %copy.58, f32[16,16,512]{2,1,0:T(8,128)S(1)} %copy-done.2, f32[64,16,512]{2,1,0:T(8,128)S(1)} %bitcast.80, f32[80,3,512]{2,1,0:T(4,128)} %copy-done.3, f32[80,22,3]{2,1,0:T(8,128)} %copy.61), kind=kLoop, calls=%fused_computation.12 | loop fusion | flops 4558400 | bytes 7293440 | tf_op jit(solution)/shard_map/concatenate | solution.py:27
  148.8 2.0 slice_add_fusion
  150.8 4.2 %slice_add_fusion.6 = f32[80,16,512]{2,1,0:T(8,128)S(1)} fusion(f32[80,16,518]{2,1,0:T(8,128)S(1)} %slice_add_fusion), kind=kLoop, calls=%fused_computation.39 | loop fusion | flops 3932160 | bytes 20971520 | tf_op jit(solution)/shard_map/add | solution.py:40
  155.0 1.6 slice.190
  158.9 2.8 %fusion.17 = (f32[8,16,512]{2,1,0:T(8,128)S(1)}, f32[8,4,16,512]{3,2,1,0:T(8,128)S(1)}, f32[8,4,16,512]{3,2,1,0:T(8,128)S(1)}) fusion(f32[8,16,512]{2,1,0:T(8,128)S(1)} %copy-done.8, pred[8,4]{1,0:T(8,128)(4,1)S(1)} %copy.63, f32[8,16,512]{2,1,0:T(8,128)S(1)} %slice-done, f32[8,8,16,512]{3,2,1,0:T(8,128)} %bitcast.81, f32[8,4]{1,0:T(8,128)S(1)} %copy.54, ...), kind=kLoop, calls=%fused_computation.116 | loop fusion | flops 3604480 | bytes 7078048 | tf_op jit(solution)/shard_map/reduce_sum | solution.py:88
  163.4 9.1 %collective-permute-done.6 = f32[8,16,512]{2,1,0:T(8,128)S(1)} collective-permute-done((f32[8,16,512]{2,1,0:T(8,128)S(1)}, f32[8,16,512]{2,1,0:T(8,128)S(1)}, u32[]{:S(2)}, u32[]{:S(2)}) %collective-permute-start.6) | collective-permute-done | bytes 262176 | tf_op jit(solution)/shard_map/ppermute | solution.py:15
  173.5 1.7 collective-permute-start.7
  175.9 4.0 %collective-permute-done.7 = bf16[2,8,16,512]{3,2,1,0:T(8,128)(2,1)S(1)} collective-permute-done((bf16[2,8,16,512]{3,2,1,0:T(8,128)(2,1)S(1)}, bf16[2,8,16,512]{3,2,1,0:T(8,128)(2,1)S(1)}, u32[]{:S(2)}, u32[]{:S(2)}) %collective-permute-start.7) | collective-permute-done | bytes 262176 | tf_op jit(solution)/shard_map/ppermute | solution.py:15
  184.0 2.4 %fusion.1 = (f32[]{:T(128)}, f32[]{:T(128)}, f32[]{:T(128)}) fusion(f32[8,4,16,512]{3,2,1,0:T(8,128)S(1)} %get-tuple-element.25, f32[8,4,16,512]{3,2,1,0:T(8,128)S(1)} %bitcast.82, f32[8,16,512]{2,1,0:T(8,128)S(1)} %copy-done.7, pred[8,4]{1,0:T(8,128)(4,1)S(1)} %copy.63, f32[8,4,16,512]{3,2,1,0:T(8,128)} %bitcast.83, f32[8,16,512]{2,1,0:T(8,128)S(1)} %get-tuple-element.22), kind=kLoop, calls=%fused_computation.47 | loop fusion | flops 3145725 | bytes 3670060 | tf_op jit(solution)/shard_map/reduce_sum | solution.py:116
  186.4 12.5 %all-reduce.1 = (f32[]{:T(128)}, f32[]{:T(128)}, f32[]{:T(128)}, f32[]{:T(128)}, f32[]{:T(128)}) all-reduce(f32[]{:T(128)} %get-tuple-element.8, f32[]{:T(128)} %get-tuple-element.7, f32[]{:T(128)} %get-tuple-element.6, f32[]{:T(128)} %get-tuple-element.5, ...), channel_id=1, replica_groups=mesh['groups'=2,'epoch'=4,'space'=2,'sub'=2] {'epoch'}, use_global_device_ids=true, to_apply=%region_11.14 | all-reduce | flops 5 | bytes 40 | tf_op jit(solution)/shard_map/psum | solution.py:110
  198.9 6.7 %all-reduce = (f32[]{:T(128)}, f32[]{:T(128)}, f32[]{:T(128)}, f32[]{:T(128)}, f32[]{:T(128)}) all-reduce(f32[]{:T(128)} %get-tuple-element.14, f32[]{:T(128)} %get-tuple-element.15, f32[]{:T(128)} %get-tuple-element.16, f32[]{:T(128)} %get-tuple-element.17, ...), channel_id=1, replica_groups=mesh['groups'=2,'epoch'=4,'space'=2,'sub'=2] {'space','sub'}, use_global_device_ids=true, to_apply=%region_12.15 | all-reduce | flops 5 | bytes 40 | tf_op jit(solution)/shard_map/psum | solution.py:109
  (90 shorter events, 30.3 us)
Async XLA Ops:
  0.6 27.9 %collective-permute-start = (bf16[2,8,64,512]{3,2,1,0:T(8,128)(2,1)}, bf16[2,8,64,512]{3,2,1,0:T(8,128)(2,1)S(1)}, u32[]{:S(2)}, u32[]{:S(2)}) collective-permute-start(bf16[2,8,64,512]{3,2,1,0:T(8,128)(2,1)} %param.10), channel_id=1, source_target_pairs={{0,12},{4,0},{8,4},{12,8},{1,13},{5,1},{9,5},{13,9},{2,14},{6,2},{... | collective-permute-start | bytes 3145736 | tf_op jit(solution)/shard_map/ppermute | solution.py:15
  51.4 2.0 copy-start.1
  74.0 5.2 %copy-start.6 = (f32[8,64,512]{2,1,0:T(8,128)S(1)}, f32[8,64,512]{2,1,0:T(8,128)}, u32[]{:S(2)}) copy-start(f32[8,64,512]{2,1,0:T(8,128)} %get-tuple-element.49) | copy-start | bytes 3145732
  80.5 7.7 %copy-start.4 = (f32[8,64,512]{2,1,0:T(8,128)S(1)}, f32[8,64,512]{2,1,0:T(8,128)}, u32[]{:S(2)}) copy-start(f32[8,64,512]{2,1,0:T(8,128)} %get-tuple-element.38) | copy-start | bytes 3145732
  89.5 7.7 %copy-start.5 = (f32[8,64,512]{2,1,0:T(8,128)S(1)}, f32[8,64,512]{2,1,0:T(8,128)}, u32[]{:S(2)}) copy-start(f32[8,64,512]{2,1,0:T(8,128)} %get-tuple-element.36) | copy-start | bytes 3145732
  98.5 3.8 %copy-start.9 = (f32[8,16,512]{2,1,0:T(8,128)S(1)}, f32[8,16,512]{2,1,0:T(8,128)}, u32[]{:S(2)}) copy-start(f32[8,16,512]{2,1,0:T(8,128)} %reduce_sum.138) | copy-start | bytes 786436
  98.5 3.8 %copy-start.10 = (f32[8,16,512]{2,1,0:T(8,128)S(1)}, f32[8,16,512]{2,1,0:T(8,128)}, u32[]{:S(2)}) copy-start(f32[8,16,512]{2,1,0:T(8,128)} %reduce_sum.139) | copy-start | bytes 786436
  101.2 1.2 copy-start.11
  101.2 1.2 copy-start.12
  101.2 1.3 copy-start.13
  101.2 1.4 copy-start.2
  102.9 8.6 %copy-start.8 = (f32[8,16,512]{2,1,0:T(8,128)S(1)}, f32[8,16,512]{2,1,0:T(8,128)}, u32[]{:S(2)}) copy-start(f32[8,16,512]{2,1,0:T(8,128)} %param.13) | copy-start | bytes 786436
  102.9 12.8 %copy-start.14 = (s32[8,4]{0,1:T(4,128)S(1)}, s32[8,4]{0,1:T(4,128)}, u32[]{:S(2)}) copy-start(s32[8,4]{0,1:T(4,128)} %param.11) | copy-start | bytes 388
  102.9 12.9 %copy-start.15 = (f32[8,4]{0,1:T(4,128)S(1)}, f32[8,4]{0,1:T(4,128)}, u32[]{:S(2)}) copy-start(f32[8,4]{0,1:T(4,128)} %param.12) | copy-start | bytes 388
  103.1 14.1 %collective-permute-start.2 = (f32[80,3,512]{2,0,1:T(8,128)S(1)}, f32[80,3,512]{2,0,1:T(8,128)}, u32[]{:S(2)}, u32[]{:S(2)}) collective-permute-start(f32[80,3,512]{2,0,1:T(8,128)S(1)} %copy.56), channel_id=1, source_target_pairs={{2,0},{3,1},{6,4},{7,5},{10,8},{11,9},{14,12},{15,13},{18,16},{19,... | collective-permute-start | bytes 1474568 | tf_op jit(solution)/shard_map/ppermute | solution.py:26
  105.5 14.8 %collective-permute-start.1 = (f32[80,3,512]{2,0,1:T(8,128)}, f32[80,3,512]{2,0,1:T(8,128)}, u32[]{:S(2)}, u32[]{:S(2)}) collective-permute-start(f32[80,3,512]{2,0,1:T(8,128)} %copy.55), channel_id=1, source_target_pairs={{0,2},{1,3},{4,6},{5,7},{8,10},{9,11},{12,14},{13,15},{16,18},{17,... | collective-permute-start | bytes 1474568 | tf_op jit(solution)/shard_map/ppermute | solution.py:23
  111.4 21.9 %collective-permute-start.5 = (f32[8,16,512]{2,1,0:T(8,128)S(1)}, f32[8,16,512]{2,1,0:T(8,128)}, u32[]{:S(2)}, u32[]{:S(2)}) collective-permute-start(f32[8,16,512]{2,1,0:T(8,128)S(1)} %copy-done.8), channel_id=1, source_target_pairs={{0,12},{4,0},{8,4},{12,8},{1,13},{5,1},{9,5},{13,9},{2,14},{6,2},{... | collective-permute-start | bytes 786440 | tf_op jit(solution)/shard_map/ppermute | solution.py:15
  121.6 1.9 copy-start.3
  125.7 12.2 %collective-permute-start.4 = (f32[80,22,3]{0,1,2:T(8,128)}, f32[80,22,3]{0,1,2:T(8,128)}, u32[]{:S(2)}, u32[]{:S(2)}) collective-permute-start(f32[80,22,3]{0,1,2:T(8,128)} %copy.60), channel_id=1, source_target_pairs={{1,0},{3,2},{5,4},{7,6},{9,8},{11,10},{13,12},{15,14},{17,16},{19,... | collective-permute-start | bytes 63368 | tf_op jit(solution)/shard_map/ppermute | solution.py:26
  129.1 10.8 %collective-permute-start.3 = (f32[80,22,3]{0,1,2:T(8,128)}, f32[80,22,3]{0,1,2:T(8,128)}, u32[]{:S(2)}, u32[]{:S(2)}) collective-permute-start(f32[80,22,3]{0,1,2:T(8,128)} %copy.59), channel_id=1, source_target_pairs={{0,1},{2,3},{4,5},{6,7},{8,9},{10,11},{12,13},{14,15},{16,17},{18,... | collective-permute-start | bytes 63368 | tf_op jit(solution)/shard_map/ppermute | solution.py:23
  155.0 2.2 %copy-start = (f32[80,16,512]{2,1,0:T(8,128)}, f32[80,16,512]{2,1,0:T(8,128)S(1)}, u32[]{:S(2)}) copy-start(f32[80,16,512]{2,1,0:T(8,128)S(1)} %slice_add_fusion.6) | copy-start | bytes 7864324
  157.2 1.6 slice-start
  162.3 10.4 %copy-start.7 = (f32[8,16,512]{2,1,0:T(8,128)S(1)}, f32[8,16,512]{2,1,0:T(8,128)}, u32[]{:S(2)}) copy-start(f32[8,16,512]{2,1,0:T(8,128)} %param.14) | copy-start | bytes 786436
  163.0 9.5 %collective-permute-start.6 = (f32[8,16,512]{2,1,0:T(8,128)S(1)}, f32[8,16,512]{2,1,0:T(8,128)S(1)}, u32[]{:S(2)}, u32[]{:S(2)}) collective-permute-start(f32[8,16,512]{2,1,0:T(8,128)S(1)} %copy.69), channel_id=1, source_target_pairs={{0,4},{4,8},{8,12},{12,0},{1,5},{5,9},{9,13},{13,1},{2,6},{6,10},{... | collective-permute-start | bytes 786440 | tf_op jit(solution)/shard_map/ppermute | solution.py:15
  173.5 6.4 %collective-permute-start.7 = (bf16[2,8,16,512]{3,2,1,0:T(8,128)(2,1)S(1)}, bf16[2,8,16,512]{3,2,1,0:T(8,128)(2,1)S(1)}, u32[]{:S(2)}, u32[]{:S(2)}) collective-permute-start(bf16[2,8,16,512]{3,2,1,0:T(8,128)(2,1)S(1)} %pad_maximum_fusion.10), channel_id=1, source_target_pairs={{0,12},{4,0},{8,4},{12,8},{1,13},{5,1},{9,5},{13,9},{2,14},{6,2},{... | collective-permute-start | bytes 786440 | tf_op jit(solution)/shard_map/ppermute | solution.py:15
